TPU v7x, 32 devices: a whole 2x2x4 slice. The times are simulated.
32 devices in a mesh: row: 8 (over y, x, core), ck: 4 (over z).
Axes of the slice: x: 2, y: 2, z: 4, core: 2. Of those that a mesh axis runs over, the one named last changes fastest.
Arguments:
- amp_tiles: bfloat16 [8, 4, 8, 16, 128, 128], P('row', 'ck'), may hold values from -6 to 6
- tile_pos: int32 [8, 4, 8, 16], P(None, 'ck'), may hold values from 0 to 2303, as said below
- tile_count: int32 [8, 4, 8], P(None, 'ck'), may hold values from 0 to 16, as said below
- cycle_integrals: bfloat16 [147456, 512], P('ck'), may hold values from -0.09375 to 0.09375
- row_gap: float32 [8192], P(('row', 'ck')), may hold values from 0.5 to 4
- col_gap: float32 [512], replicated, may hold values from 0.5 to 4
Outputs:
- new_amp: bfloat16 [8192, 512], P(('row', 'ck'))
Inputs may be any that keep to these rules, and one draw needn't show every extreme that they name: `tile_pos`: slots 0 to tile_count - 1 of each list are live, the others hold no tile. Within one ck group and one row owner all slots' positions are distinct. `tile_count`: in every ck group one row owner receives 16 live tiles from every storage owner.
All inputs are finite; a program needn't handle non-finite values.
Results may differ from a plain program's by a relative error of at most 0.001.
Values may be sent and summed in bfloat16 or wider, within the bound.
No kernel may reach another device: no remote copies, remote signals or barrier semaphores. Data moves between devices by JAX's collectives and lax.ppermute only.
A program may use at most 320 MiB of HBM per device.

v0:
```python
import jax
import jax.numpy as jnp
from jax import lax
from jax.sharding import PartitionSpec as P

TILE = 128
KT_DEV = 288
CAP = 16


def slot_products(amp_slots, positions, integrals):
    tile_width = amp_slots.shape[-1]
    blocks = integrals.reshape(-1, tile_width, integrals.shape[-1])
    picked = blocks[positions % blocks.shape[0]]
    return jnp.einsum("mrk,mkc->mrc", amp_slots, picked, preferred_element_type=jnp.float32)


def row_terms(products, tile_ids, live_mask, row_count):
    tile_width = products.shape[1]
    segment_total = row_count // tile_width
    inside = live_mask & (tile_ids >= 0) & (tile_ids < segment_total)
    target = jnp.where(inside, tile_ids, segment_total)
    summed = jax.ops.segment_sum(products, target, num_segments=segment_total + 1)[:segment_total]
    return summed.reshape(row_count, products.shape[2])


def on_device(amp_tiles, tile_pos, tile_count, cycle_integrals, row_gap, col_gap):
    my_row = lax.axis_index("row")
    slot_range = jnp.arange(CAP)
    share_rows = row_gap.shape[0]
    received = lax.all_to_all(amp_tiles, "row", split_axis=2, concat_axis=0, tiled=True)
    amp_slots = received.reshape(-1, TILE, TILE)
    positions = lax.dynamic_index_in_dim(tile_pos, my_row, 2, keepdims=False).reshape(-1)
    counts = lax.dynamic_index_in_dim(tile_count, my_row, 2, keepdims=False).reshape(-1)
    live_mask = (slot_range[None, :] < counts[:, None]).reshape(-1)
    tile_ids = positions // KT_DEV
    products = slot_products(amp_slots, positions, cycle_integrals)
    reduced = lax.psum_scatter(
        row_terms(products, tile_ids, live_mask, lax.axis_size("ck") * share_rows),
        "ck",
        scatter_dimension=0,
        tiled=True,
    )
    quotient = (reduced / (row_gap[:, None] + col_gap[None, :])).astype(jnp.bfloat16)
    return lax.all_to_all(quotient, "row", split_axis=0, concat_axis=0, tiled=True)


def solution(mesh):
    return jax.shard_map(
        on_device,
        mesh=mesh,
        in_specs=(
            P("row", "ck", None, None, None, None),
            P(None, "ck", None, None),
            P(None, "ck", None),
            P("ck", None),
            P(("row", "ck")),
            P(),
        ),
        out_specs=P(("row", "ck"), None),
        check_vma=False,
    )
```

profile of v0, /device:TPU:0, one launch (start us, length us, event | category | flops | bytes accessed | tf_op | source)
XLA Modules:
  0.0 227.3 jit_solution(11846260106764262696)
XLA Ops:
  6.5 5.3 %all-to-all-start = ((bf16[1,1,8,16,128,128]{5,4,3,1,0,2:T(8,128)(2,1)}), bf16[1,1,8,16,128,128]{5,4,3,1,0,2:T(8,128)(2,1)}, u32[]{:S(2)}, u32[]{:S(2)}) async-start(bf16[1,1,8,16,128,128]{5,4,3,1,0,2:T(8,128)(2,1)} %bitcast.16), calls=%async_computation | async-start | bytes 8388608 | tf_op jit(solution)/shard_map/all_to_all | solution.py:31
  11.9 0.0 reduce-scatter.2.cloned.1.call-start
  11.9 0.8 remainder_reduce_fusion
  12.7 0.1 div.20
  12.8 0.1 rem.30
  12.9 0.3 dynamic-slice_reduce_fusion
  13.2 0.1 iota_compare_fusion
  13.3 0.1 lt.66
  13.4 0.8 compare_reduce_fusion
  14.2 0.1 ne.52
  14.3 12.6 %gather_fusion = bf16[128,128,512]{2,1,0:T(8,128)(2,1)} fusion(bf16[288,128,512]{2,1,0:T(8,128)(2,1)} %bitcast.15, s32[1024]{0:T(1024)S(1)} %pad_clamp_fusion), kind=kCustom, calls=%fused_computation | custom fusion | bytes 33554944 | tf_op jit(solution)/shard_map/gather | solution.py:14
  26.9 34.2 %all-to-all-done = bf16[1,1,8,16,128,128]{5,4,3,1,0,2:T(8,128)(2,1)} async-done(((bf16[1,1,8,16,128,128]{5,4,3,1,0,2:T(8,128)(2,1)}), bf16[1,1,8,16,128,128]{5,4,3,1,0,2:T(8,128)(2,1)}, u32[]{:S(2)}, u32[]{:S(2)}) %all-to-all-start) | async-done | bytes 4194336 | tf_op jit(solution)/shard_map/all_to_all | solution.py:31
  61.1 22.3 %convolution_bitcast_fusion = f32[128,128,512]{1,2,0:T(8,128)} fusion(bf16[128,128,512]{2,1,0:T(8,128)(2,1)} %gather_fusion, bf16[128,128,128]{2,1,0:T(8,128)(2,1)} %bitcast.4), kind=kOutput, calls=%fused_computation.2 | convolution fusion | flops 2147483648 | bytes 54525952 | tf_op jit(solution)/shard_map/mrk,mkc->mrc/dot_general | solution.py:15
  83.4 33.4 %copy.12 = f32[128,128,512]{2,1,0:T(8,128)} copy(f32[128,128,512]{1,2,0:T(8,128)} %convolution_bitcast_fusion) | data formatting | bytes 67108864 | tf_op jit(solution)/shard_map/mrk,mkc->mrc/dot_general | solution.py:15
  116.8 0.3 broadcast_in_dim.3
  117.1 0.0 copy-start.2
  117.1 0.0 copy-start.1
  117.2 45.1 %scatter_fusion = f32[9,128,512]{2,1,0:T(8,128)S(1)} fusion(f32[9,128,512]{2,1,0:T(8,128)S(1)} %broadcast_in_dim.3, s32[128]{0:T(128)S(1)} %get-tuple-element.8, f32[128,128,512]{2,1,0:T(8,128)} %copy.12), kind=kCustom, calls=%fused_computation.1 | custom fusion | flops 8388608 | bytes 100663808 | tf_op jit(solution)/shard_map/scatter-add | solution.py:23
  162.3 1.6 slice.6
  163.9 0.0 reduce-scatter.2.cloned.1.call-update
  163.9 44.3 %reduce-scatter.2.cloned.1.call-done = f32[256,512]{1,0:T(8,128)} async-done(((f32[1024,512]{1,0:T(8,128)}), f32[256,512]{1,0:T(8,128)}) %reduce-scatter.2.cloned.1.call-update) | async-done | bytes 524304 | tf_op jit(solution)/shard_map/reduce_scatter | solution.py:38
  208.2 1.2 divide_convert_fusion
  209.4 10.4 %all_to_all.21 = bf16[8,32,512]{2,1,0:T(8,128)(2,1)S(1)} all-to-all(bf16[8,32,512]{2,1,0:T(8,128)(2,1)S(1)} %bitcast.17), channel_id=1, replica_groups=mesh['row'=8,'ck'=4] {'row'}, dimensions={0} | all-to-all | bytes 524288 | tf_op jit(solution)/shard_map/all_to_all | solution.py:45
  219.7 0.7 copy.16
  (8 shorter events, 0.0 us)
Async XLA Ops:
  6.5 6.4 %copy-start = (s32[8,1,8]{2,1,0:T(1,128)S(1)}, s32[8,1,8]{2,1,0:T(1,128)}, u32[]{:S(2)}) copy-start(s32[8,1,8]{2,1,0:T(1,128)} %param.8) | copy-start | bytes 772
  6.5 54.5 %all-to-all-start = ((bf16[1,1,8,16,128,128]{5,4,3,1,0,2:T(8,128)(2,1)}), bf16[1,1,8,16,128,128]{5,4,3,1,0,2:T(8,128)(2,1)}, u32[]{:S(2)}, u32[]{:S(2)}) async-start(bf16[1,1,8,16,128,128]{5,4,3,1,0,2:T(8,128)(2,1)} %bitcast.16), calls=%async_computation | async-start | bytes 8388608 | tf_op jit(solution)/shard_map/all_to_all | solution.py:31
  11.9 196.3 %reduce-scatter.2.cloned.1.call-start = ((), (), s32[]{:S(2)}) async-start(), calls=%async_computation.3 | async-start | bytes 2621440 | tf_op jit(solution)/shard_map/reduce_scatter | solution.py:38
  117.1 91.1 %copy-start.2 = (f32[512]{0:T(512)S(1)}, f32[512]{0:T(512)}, u32[]{:S(2)}) copy-start(f32[512]{0:T(512)} %param.11) | copy-start | bytes 6148
  117.1 91.1 %copy-start.3 = (f32[256]{0:T(256)S(1)}, f32[256]{0:T(256)}, u32[]{:S(2)}) copy-start(f32[256]{0:T(256)} %param.10) | copy-start | bytes 3076
  117.1 103.3 %copy-start.1 = (s32[8,1,8]{2,1,0:T(1,128)S(1)}, s32[8,1,8]{2,1,0:T(1,128)}, u32[]{:S(2)}) copy-start(s32[8,1,8]{2,1,0:T(1,128)} %param.8) | copy-start | bytes 772
Sparse Core Ops, SparseCore 0:
  164.0 44.0 reduce-scatter.1
where the time goes:
time: 229 us; the launch traced here: 227 us
  waiting for transfers between devices  78.5 us (34%)
  local copies, waits for them, and re-layouts  49.3 us (22%)
  other arithmetic  48 us (21%)
  matrix products  22.3 us (10%)
  between operations  13.5 us (6%)
  blocking collectives  10.4 us (5%)
  starting transfers between devices  5.37 us (2%)
    scatter-add x1, other arithmetic, row_terms(): jax.ops.segment_sum(products, target, num_segments=segment_total + 1)  45.1 us
    reduce_scatter x1, waiting for transfers between devices, on_device(): lax.psum_scatter(row_terms(products, tile_ids, live_mask, lax.axis_size('...  44.3 us
    all_to_all x1, waiting for transfers between devices, on_device(): lax.all_to_all(amp_tiles, 'row', split_axis=2, concat_axis=0, tiled=True)  34.2 us
    dot_general x1, local copies, waits for them, and re-layouts, slot_products(): jnp.einsum('mrk,mkc->mrc', amp_slots, picked, preferred_element_type=jnp....  33.4 us
    dot_general x1, matrix products, slot_products(): jnp.einsum('mrk,mkc->mrc', amp_slots, picked, preferred_element_type=jnp....  22.3 us
    gather x1, local copies, waits for them, and re-layouts, slot_products(): picked = blocks[positions % blocks.shape[0]]  12.6 us
    all_to_all x1, blocking collectives, on_device(): lax.all_to_all(quotient, 'row', split_axis=0, concat_axis=0, tiled=True)  10.4 us
    all_to_all x1, starting transfers between devices, on_device(): lax.all_to_all(amp_tiles, 'row', split_axis=2, concat_axis=0, tiled=True)  5.33 us
  transfers between devices with their start and end apart: 2, of which 2 were waited for; matrix products, arithmetic and copies ran while one was open for 7% of the time, Pallas kernels for 0%

commit v1 on v0

--- a/solution.py
+++ b/solution.py
@@ -28,7 +28,9 @@
     my_row = lax.axis_index("row")
     slot_range = jnp.arange(CAP)
     share_rows = row_gap.shape[0]
-    received = lax.all_to_all(amp_tiles, "row", split_axis=2, concat_axis=0, tiled=True)
+    pieces = jnp.split(amp_tiles, lax.axis_size("row"), axis=2)
+    incoming = lax.all_to_all(jnp.stack(pieces), "row", 0, 0)
+    received = jnp.concatenate(incoming, axis=0)
     amp_slots = received.reshape(-1, TILE, TILE)
     positions = lax.dynamic_index_in_dim(tile_pos, my_row, 2, keepdims=False).reshape(-1)
     counts = lax.dynamic_index_in_dim(tile_count, my_row, 2, keepdims=False).reshape(-1)

time: 229 us -> 206 us (0.90)
  local copies, waits for them, and re-layouts: 49.3 us -> 31 us
  matrix products: 22.3 us -> 17.9 us
    dot_general x1 -> x0, local copies, waits for them, and re-layouts: 33.4 us -> none  [slot_products(): jnp.einsum('mrk,mkc->mrc', amp_slots, picked, preferred_element_type=jnp....]
    unnamed x9 -> x16, local copies, waits for them, and re-layouts: 0.73 us -> 14 us
    dot_general x1, matrix products: 22.3 us -> 17.9 us  [slot_products(): jnp.einsum('mrk,mkc->mrc', amp_slots, picked, preferred_element_type=jnp....]
where the time goes in v1:
time: 206 us; the launch traced here: 204 us
  waiting for transfers between devices  78.5 us (38%)
  other arithmetic  48 us (23%)
  local copies, waits for them, and re-layouts  31 us (15%)
  matrix products  17.9 us (9%)
  between operations  13.5 us (7%)
  blocking collectives  10.3 us (5%)
  starting transfers between devices  5.24 us (3%)
    scatter-add x1, other arithmetic, row_terms(): jax.ops.segment_sum(products, target, num_segments=segment_total + 1)  45.1 us
    reduce_scatter x1, waiting for transfers between devices, on_device(): lax.psum_scatter(row_terms(products, tile_ids, live_mask, lax.axis_size('...  44.3 us
    all_to_all x1, waiting for transfers between devices, on_device(): incoming = lax.all_to_all(jnp.stack(pieces), 'row', 0, 0)  34.2 us
    dot_general x1, matrix products, slot_products(): jnp.einsum('mrk,mkc->mrc', amp_slots, picked, preferred_element_type=jnp....  17.9 us
    unnamed x16, local copies, waits for them, and re-layouts  14 us
    gather x1, local copies, waits for them, and re-layouts, slot_products(): picked = blocks[positions % blocks.shape[0]]  12.6 us
    all_to_all x1, blocking collectives, on_device(): lax.all_to_all(quotient, 'row', split_axis=0, concat_axis=0, tiled=True)  10.3 us
    all_to_all x1, starting transfers between devices, on_device(): incoming = lax.all_to_all(jnp.stack(pieces), 'row', 0, 0)  5.2 us
  transfers between devices with their start and end apart: 2, of which 2 were waited for; matrix products, arithmetic and copies ran while one was open for 7% of the time, Pallas kernels for 0%

profile of v1, /device:TPU:0, one launch (start us, length us, event | category | flops | bytes accessed | tf_op | source)
XLA Modules:
  0.0 204.5 jit_solution(6590056450716323353)
XLA Ops:
  6.5 1.9 bitcast_dynamic-update-slice_fusion.7
  8.4 1.9 bitcast_dynamic-update-slice_fusion.6
  10.3 1.9 bitcast_dynamic-update-slice_fusion.5
  12.2 1.9 bitcast_dynamic-update-slice_fusion.4
  14.1 1.9 bitcast_dynamic-update-slice_fusion.3
  16.0 1.9 bitcast_dynamic-update-slice_fusion.2
  17.9 1.9 bitcast_dynamic-update-slice_fusion.1
  19.8 1.9 bitcast_dynamic-update-slice_fusion
  21.7 5.2 %all-to-all-start = ((bf16[8,1,1,1,16,128,128]{6,5,4,3,2,1,0:T(8,128)(2,1)}), bf16[8,1,1,1,16,128,128]{6,5,4,3,2,1,0:T(8,128)(2,1)}, u32[]{:S(2)}, u32[]{:S(2)}) async-start(bf16[8,1,1,1,16,128,128]{6,5,4,3,2,1,0:T(8,128)(2,1)} %bitcast_dynamic-update-slice_fusion), calls=%async_computation | async-start | bytes 8388608 | tf_op jit(solution)/shard_map/all_to_all | solution.py:32
  27.0 0.8 remainder_reduce_fusion
  27.9 0.3 dynamic-slice_reduce_fusion
  28.3 0.1 lt.66
  28.4 0.8 compare_reduce_fusion
  29.2 0.1 ne.52
  29.3 12.6 %gather_fusion = bf16[128,128,512]{2,1,0:T(8,128)(2,1)} fusion(bf16[288,128,512]{2,1,0:T(8,128)(2,1)} %bitcast.28, s32[1024]{0:T(1024)S(1)} %pad_clamp_fusion), kind=kCustom, calls=%fused_computation | custom fusion | bytes 33554944 | tf_op jit(solution)/shard_map/gather | solution.py:14
  41.9 34.2 %all-to-all-done = bf16[8,1,1,1,16,128,128]{6,5,4,3,2,1,0:T(8,128)(2,1)} async-done(((bf16[8,1,1,1,16,128,128]{6,5,4,3,2,1,0:T(8,128)(2,1)}), bf16[8,1,1,1,16,128,128]{6,5,4,3,2,1,0:T(8,128)(2,1)}, u32[]{:S(2)}, u32[]{:S(2)}) %all-to-all-start) | async-done | bytes 4194336 | tf_op jit(solution)/shard_map/all_to_all | solution.py:32
  76.1 17.9 %fusion.2 = f32[128,128,512]{2,1,0:T(8,128)} fusion(bf16[128,128,128]{2,1,0:T(8,128)(2,1)} %bitcast.9, bf16[128,128,512]{2,1,0:T(8,128)(2,1)} %gather_fusion), kind=kOutput, calls=%fused_computation.24 | convolution fusion | flops 2147483648 | bytes 54525952 | tf_op jit(solution)/shard_map/mrk,mkc->mrc/dot_general | solution.py:15
  94.0 0.3 broadcast_in_dim.3
  94.3 45.1 %scatter_fusion = f32[9,128,512]{2,1,0:T(8,128)S(1)} fusion(f32[9,128,512]{2,1,0:T(8,128)S(1)} %broadcast_in_dim.3, s32[128]{0:T(128)S(1)} %get-tuple-element.8, f32[128,128,512]{2,1,0:T(8,128)} %fusion.2), kind=kCustom, calls=%fused_computation.1 | custom fusion | flops 8388608 | bytes 100663808 | tf_op jit(solution)/shard_map/scatter-add | solution.py:23
  139.4 1.6 slice.6
  141.1 44.3 %reduce-scatter.2.cloned.1.call-done = f32[256,512]{1,0:T(8,128)} async-done(((f32[1024,512]{1,0:T(8,128)}), f32[256,512]{1,0:T(8,128)}) %reduce-scatter.2.cloned.1.call-update) | async-done | bytes 524304 | tf_op jit(solution)/shard_map/reduce_scatter | solution.py:40
  185.4 1.2 divide_convert_fusion
  186.6 10.3 %all_to_all.17 = bf16[8,32,512]{2,1,0:T(8,128)(2,1)S(1)} all-to-all(bf16[8,32,512]{2,1,0:T(8,128)(2,1)S(1)} %bitcast.29), channel_id=1, replica_groups=mesh['row'=8,'ck'=4] {'row'}, dimensions={0} | all-to-all | bytes 524288 | tf_op jit(solution)/shard_map/all_to_all | solution.py:47
  196.9 0.7 copy.16
  (15 shorter events, 0.3 us)
Async XLA Ops:
  6.5 21.4 %copy-start = (s32[8,1,8]{2,1,0:T(1,128)S(1)}, s32[8,1,8]{2,1,0:T(1,128)}, u32[]{:S(2)}) copy-start(s32[8,1,8]{2,1,0:T(1,128)} %param.8) | copy-start | bytes 772
  21.7 54.4 %all-to-all-start = ((bf16[8,1,1,1,16,128,128]{6,5,4,3,2,1,0:T(8,128)(2,1)}), bf16[8,1,1,1,16,128,128]{6,5,4,3,2,1,0:T(8,128)(2,1)}, u32[]{:S(2)}, u32[]{:S(2)}) async-start(bf16[8,1,1,1,16,128,128]{6,5,4,3,2,1,0:T(8,128)(2,1)} %bitcast_dynamic-update-slice_fusion), calls=%async_computation | async-start | bytes 8388608 | tf_op jit(solution)/shard_map/all_to_all | solution.py:32
  26.9 158.5 %reduce-scatter.2.cloned.1.call-start = ((), (), s32[]{:S(2)}) async-start(), calls=%async_computation.3 | async-start | bytes 2621440 | tf_op jit(solution)/shard_map/reduce_scatter | solution.py:40
  94.3 103.3 %copy-start.1 = (s32[8,1,8]{2,1,0:T(1,128)S(1)}, s32[8,1,8]{2,1,0:T(1,128)}, u32[]{:S(2)}) copy-start(s32[8,1,8]{2,1,0:T(1,128)} %param.8) | copy-start | bytes 772
  139.4 46.0 %copy-start.2 = (f32[512]{0:T(512)S(1)}, f32[512]{0:T(512)}, u32[]{:S(2)}) copy-start(f32[512]{0:T(512)} %param.11) | copy-start | bytes 6148
  139.4 45.9 %copy-start.3 = (f32[256]{0:T(256)S(1)}, f32[256]{0:T(256)}, u32[]{:S(2)}) copy-start(f32[256]{0:T(256)} %param.10) | copy-start | bytes 3076
Sparse Core Ops, SparseCore 0:
  141.2 44.0 reduce-scatter.1
